TPU v7x, 128 devices: a whole 4x4x4 slice. The times are simulated.
128 devices in a mesh: group: 4 (over x), bulk: 32 (over z, y, core).
Axes of the slice: x: 4, y: 4, z: 4, core: 2. Of those that a mesh axis runs over, the one named last changes fastest.
Arguments:
- rhs: float32 [512, 64, 128], P(('group', 'bulk')), may hold values from -90 to 90, as said below
- diag_tiles: float32 [512, 128, 128], P(('group', 'bulk')), may hold values from -0.06 to 0.06
- offdiag_blocks: float32 [512, 11, 128, 128], P(('group', 'bulk')), may hold values from -0.026 to 0.026
- coupling: float32 [256, 4, 128, 128], P(('group', 'bulk')), may hold values from -0.05 to 0.05, as said below
- col_index: int32 [512, 11], replicated, may hold values from 0 to 511, as said below
- load: int32 [512], replicated, may hold values from 3 to 11
- new_slot: int32 [512], replicated, may hold values from 0 to 511, as said below
Outputs:
- solution_out: float32 [512, 64, 128], P(('group', 'bulk'))
- residual_out: float32 [512, 64, 128], P(('group', 'bulk'))
Inputs may be any that keep to these rules, and one draw needn't show every extreme that they name: `rhs`: made of random entries times scales of the rows and of the columns. `coupling`: entry [d * 2 + k, h] is the transpose of entry [(h * 32 + d % 32) * 2 + k, d // 32]. `col_index`: for each part g and each tile position t, the column t of the 128 block rows of part g is a permutation of that part's slots g * 128 to (g + 1) * 128 - 1. Of the 44 entries of the 4 block rows of one device (slots d * 4 to (d + 1) * 4 - 1), at most 2 name slots of any one device, and exactly 2 name slots of some device. `new_slot`: A permutation. On every device exactly one block row moves, from a slot k with 2 <= k % 4; it stays in its part, goes from owner b to owner b XOR m, where m (1 to 31) is one number for the whole part, and takes the slot that the moving row of that device leaves.
All inputs are finite; a program needn't handle non-finite values.
Results may differ from a plain program's by a relative error of at most 0.0003.
Values sent between devices are 32-bit elements; how exact they have to be, the bound alone decides.
A program may use at most 64 MiB of HBM per device.

v0:
```python
import jax
import jax.numpy as jnp
from jax import lax
from jax.sharding import PartitionSpec as P

highest = lax.Precision.HIGHEST
diagonal_shift = 4.0


def chol_apply(matrix, right):
    factor = jnp.linalg.cholesky(matrix)
    middle = lax.linalg.triangular_solve(factor, right, left_side=True, lower=True)
    return lax.linalg.triangular_solve(factor, middle, left_side=True, lower=True, transpose_a=True)


def gram(left, right):
    return jnp.einsum("snt,smt->nm", left, right, precision=highest)


def sym(m):
    return 0.5 * (m + m.T)


def mm(a, b):
    return jnp.dot(a, b, precision=highest)


def off_part(vectors, diag, masked, column_ids, coupling):
    boundary_rows = coupling.shape[0]
    part_count = coupling.shape[1]
    border = lax.all_gather(vectors[:boundary_rows], "group", axis=0, tiled=True)
    own = jnp.einsum("rnj,rij->rni", vectors, diag, precision=highest)
    returned = jnp.einsum("rni,rkij->rknj", vectors, masked, precision=highest)
    panel = lax.all_gather(vectors, "bulk", axis=0, tiled=True)
    picked = panel[column_ids]
    own = own + jnp.einsum("rknj,rkij->rni", picked, masked, precision=highest)
    border = border.reshape((part_count, boundary_rows) + vectors.shape[1:])
    crossed = jnp.einsum("khij,hknj->kni", coupling, border, precision=highest)
    return (own.at[:boundary_rows].add(crossed), returned.reshape((-1,) + vectors.shape[1:]), panel)


def coefficients(n0, n1, n2, n3):
    n = n0.shape[0]
    eye = jnp.eye(n, dtype=n0.dtype)
    n0, n1, n2, n3 = (sym(n0), sym(n1), sym(n2), sym(n3))
    delta = chol_apply(diagonal_shift * n0 + n1, n1)
    alpha = (eye - delta) / diagonal_shift
    b = -alpha
    cross = mm(delta.T, mm(n1, b))
    gram_new = sym(mm(delta.T, mm(n0, delta)) + cross + cross.T + mm(b.T, mm(n2, b)))
    beta = chol_apply(n0, gram_new)
    a = delta + beta
    c1 = mm(a.T, mm(n1, b))
    c2 = mm(a.T, mm(n2, b))
    pp = mm(a.T, mm(n0, a)) + c1 + c1.T + mm(b.T, mm(n2, b))
    pep = mm(a.T, mm(n1, a)) + c2 + c2.T + mm(b.T, mm(n3, b))
    alpha2 = chol_apply(sym(diagonal_shift * pp + pep), gram_new)
    ba = mm(b, alpha2)
    aa = mm(a, alpha2)
    sol = (alpha + aa, ba)
    res = (delta - diagonal_shift * aa, b - diagonal_shift * ba - aa, -ba)
    return (sol, res)


def local(rhs, diag_tiles, offdiag_blocks, coupling, col_index, load, new_slot):
    row_count = rhs.shape[0]
    off_count = offdiag_blocks.shape[1]
    bulk_count = lax.axis_size("bulk")
    group_rows = row_count * bulk_count
    group_base = lax.axis_index("group") * group_rows
    first = lax.axis_index("bulk") * row_count
    cols = lax.dynamic_slice_in_dim(col_index, group_base, group_rows) - group_base
    moved = lax.dynamic_slice_in_dim(new_slot, group_base, group_rows) - group_base
    loads = lax.dynamic_slice_in_dim(load, group_base + first, row_count)
    my_cols = lax.dynamic_slice_in_dim(cols, first, row_count)
    my_new = lax.dynamic_slice_in_dim(moved, first, row_count)
    tile_ids = jnp.arange(off_count, dtype=jnp.int32)
    mask = (tile_ids[None, :] < loads[:, None]).astype(jnp.float32)
    masked = offdiag_blocks * mask[:, :, None, None]
    u0 = rhs
    own, returned, panel0 = off_part(u0, diag_tiles, masked, my_cols, coupling)
    buffer = jax.ops.segment_sum(returned, my_cols.reshape(-1), num_segments=group_rows)
    u1 = own + lax.psum_scatter(buffer, "bulk", scatter_dimension=0, tiled=True)
    own, returned, panel1 = off_part(u1, diag_tiles, masked, my_cols, coupling)
    ids = jnp.concatenate([moved[my_cols.reshape(-1)], my_new])
    buffer = jax.ops.segment_sum(jnp.concatenate([returned, own]), ids, num_segments=group_rows)
    u2 = lax.psum_scatter(buffer, "bulk", scatter_dimension=0, tiled=True)
    inverse = jnp.zeros_like(moved).at[moved].set(jnp.arange(group_rows, dtype=jnp.int32))
    mine = lax.dynamic_slice_in_dim(inverse, first, row_count)
    v0, v1 = (panel0[mine], panel1[mine])
    grams = jnp.stack([gram(v0, v0), gram(v0, v1), gram(v1, v1), gram(v1, u2)])
    grams = lax.psum(grams, ("group", "bulk"))
    sol, res = coefficients(grams[0], grams[1], grams[2], grams[3])
    basis = jnp.concatenate([v0, v1, u2], axis=1)
    zero = jnp.zeros_like(sol[0])
    weights = jnp.concatenate(
        [jnp.concatenate(sol + (zero,), axis=0), jnp.concatenate(res, axis=0)], axis=1
    )
    out = jnp.einsum("mn,smt->snt", weights, basis, precision=highest)
    n = rhs.shape[1]
    return (out[:, :n], out[:, n:])


def solution(mesh):
    return jax.shard_map(
        local,
        mesh=mesh,
        in_specs=(
            P(("group", "bulk"), None, None),
            P(("group", "bulk"), None, None),
            P(("group", "bulk"), None, None, None),
            P(("group", "bulk"), None, None, None),
            P(),
            P(),
            P(),
        ),
        out_specs=(P(("group", "bulk"), None, None), P(("group", "bulk"), None, None)),
        check_vma=False,
    )
```

profile of v0, /device:TPU:1, one launch (start us, length us, event | category | flops | bytes accessed | tf_op | source)
XLA Modules:
  0.0 494.6 jit_solution(10182201475086260046)
XLA Ops:
  7.2 0.7 all-gather.3.cloned.1.call-update
  8.0 0.8 compare_select_fusion
  8.9 0.8 dynamic_slice.22
  9.8 3.8 fusion.4
  13.5 2.5 broadcast.140.clone
  16.0 6.9 %scatter_fusion = f32[128,64,128]{2,1,0:T(8,128)} fusion(f32[128,64,128]{2,1,0:T(8,128)} %broadcast.140.clone, s32[44]{0:T(128)S(1)} %reshape.206, f32[44,64,128]{2,1,0:T(8,128)S(1)} %bitcast.248), kind=kCustom, calls=%fused_computation.6 | custom fusion | flops 360448 | bytes 4325552 | tf_op jit(solution)/shard_map/scatter-add | solution.py:82
  23.0 0.8 copy-done.4
  24.4 0.7 copy.72
  25.1 0.8 reshape.166
  25.9 12.7 %all_gather.13 = f32[8,64,128]{2,1,0:T(8,128)} all-gather(f32[2,64,128]{2,1,0:T(8,128)} %slice.81), channel_id=1, replica_groups=mesh['group'=4,'bulk'=32] {'group'}, dimensions={0}, use_global_device_ids=true | all-gather | bytes 327680 | tf_op jit(solution)/shard_map/all_gather | solution.py:31
  38.5 21.5 %all-gather.3.cloned.1.call-done = f32[128,64,128]{2,1,0:T(8,128)} async-done(((f32[4,64,128]{2,1,0:T(8,128)}), f32[128,64,128]{2,1,0:T(8,128)}) %all-gather.3.cloned.1.call-update) | async-done | bytes 4194320 | tf_op jit(solution)/shard_map/all_gather | solution.py:34
  60.1 4.0 gather_fusion.1
  64.1 4.8 fusion.12
  68.9 1.3 convolution_add_fusion.1
  70.2 2.1 fusion.21
  72.4 71.0 %reduce-scatter.3.cloned.1.call-done = f32[4,64,128]{2,1,0:T(8,128)} async-done(((f32[128,64,128]{2,1,0:T(8,128)}), f32[4,64,128]{2,1,0:T(8,128)}) %reduce-scatter.3.cloned.1.call-update) | async-done | bytes 131088 | tf_op jit(solution)/shard_map/reduce_scatter | solution.py:83
  143.4 1.6 add.181
  145.2 0.8 compare_select_fusion.3
  146.0 0.8 gather_fusion.3
  146.9 0.8 slice.102
  147.7 10.6 %all_gather.15 = f32[8,64,128]{2,1,0:T(8,128)} all-gather(f32[2,64,128]{2,1,0:T(8,128)S(1)} %slice.102), channel_id=1, replica_groups=mesh['group'=4,'bulk'=32] {'group'}, dimensions={0}, use_global_device_ids=true | all-gather | bytes 327680 | tf_op jit(solution)/shard_map/all_gather | solution.py:31
  158.3 4.1 fusion.2
  162.4 31.4 %all-gather.5.cloned.1.call-done = f32[128,64,128]{2,1,0:T(8,128)} async-done(((f32[4,64,128]{2,1,0:T(8,128)}), f32[128,64,128]{2,1,0:T(8,128)}) %all-gather.5.cloned.1.call-update) | async-done | bytes 4194320 | tf_op jit(solution)/shard_map/all_gather | solution.py:34
  193.8 3.9 gather_fusion.4
  197.7 4.9 fusion.15
  203.3 0.7 fusion.19
  204.1 2.5 broadcast.140
  206.6 6.9 %scatter_fusion.1 = f32[128,64,128]{2,1,0:T(8,128)} fusion(f32[128,64,128]{2,1,0:T(8,128)} %broadcast.140, s32[48]{0:T(128)S(1)} %pad_add_fusion, f32[48,64,128]{2,1,0:T(8,128)S(1)} %pad_maximum_fusion), kind=kCustom, calls=%fused_computation.7 | custom fusion | flops 393216 | bytes 4718784 | tf_op jit(solution)/shard_map/scatter-add | solution.py:86
  213.6 1.2 scatter_custom_fusion
  214.9 2.7 gather_fusion
  217.9 2.7 gather_fusion.2
  221.1 72.2 %reduce-scatter.5.cloned.1.call-done = f32[4,64,128]{2,1,0:T(8,128)} async-done(((f32[128,64,128]{2,1,0:T(8,128)}), f32[4,64,128]{2,1,0:T(8,128)}) %reduce-scatter.5.cloned.1.call-update) | async-done | bytes 131088 | tf_op jit(solution)/shard_map/reduce_scatter | solution.py:87
  293.4 1.2 convolution_bitcast_fusion.3
  294.5 0.7 pad_maximum_fusion.1
  295.2 146.3 %all-reduce.2.cloned.1.call-done = f32[4,64,64]{2,1,0:T(8,128)} async-done(((f32[4,64,64]{2,1,0:T(8,128)}), f32[4,64,64]{2,1,0:T(8,128)}) %all-reduce.2.cloned.1.call-update) | async-done | bytes 65552 | tf_op jit(solution)/shard_map/psum | solution.py:92
  441.6 0.8 slice_bitcast_fusion.2
  442.5 0.8 multiply_add_fusion
  443.6 5.9 %cholesky.59 = f32[64,64]{1,0:T(8,128)S(1)} custom-call(f32[64,64]{1,0:T(8,128)S(1)} %copy.82), custom_call_target="Cholesky" | custom-call | tf_op jit(solution)/shard_map/jit(cholesky)/cholesky | solution.py:11
  450.1 0.7 fusion.41
  450.8 4.9 custom-call.13
  456.7 5.9 %cholesky.70 = f32[64,64]{1,0:T(8,128)S(1)} custom-call(f32[64,64]{1,0:T(8,128)S(1)} %copy.85), custom_call_target="Cholesky" | custom-call | tf_op jit(solution)/shard_map/jit(cholesky)/cholesky | solution.py:11
  463.9 4.9 custom-call.15
  468.8 1.0 fusion.67
  471.9 1.0 fusion.45
  473.9 5.8 %cholesky.81 = f32[64,64]{1,0:T(8,128)S(1)} custom-call(f32[64,64]{1,0:T(8,128)S(1)} %fusion.51), custom_call_target="Cholesky" | custom-call | tf_op jit(solution)/shard_map/jit(cholesky)/cholesky | solution.py:11
  480.5 0.7 fusion.43
  481.1 4.9 custom-call.17
  487.4 0.7 fusion.103
  (96 shorter events, 11.4 us)
Async XLA Ops:
  7.2 63.1 %copy-start = (f32[2,4,128,128]{3,2,1,0:T(8,128)S(1)}, f32[2,4,128,128]{3,2,1,0:T(8,128)}, u32[]{:S(2)}) copy-start(f32[2,4,128,128]{3,2,1,0:T(8,128)} %param.19) | copy-start | bytes 1572868
  7.2 52.9 %all-gather.3.cloned.1.call-start = ((), (), s32[]{:S(2)}) async-start(), calls=%async_computation.2 | async-start | bytes 4325376 | tf_op jit(solution)/shard_map/all_gather | solution.py:34
  7.9 135.5 %reduce-scatter.3.cloned.1.call-start = ((), (), s32[]{:S(2)}) async-start(), calls=%async_computation.3 | async-start | bytes 4325376 | tf_op jit(solution)/shard_map/reduce_scatter | solution.py:83
  22.9 0.9 copy-start.4
  22.9 41.2 %copy-start.1 = (f32[4,11,128,128]{3,2,1,0:T(8,128)S(1)}, f32[4,11,128,128]{3,2,1,0:T(8,128)}, u32[]{:S(2)}) copy-start(f32[4,11,128,128]{3,2,1,0:T(8,128)} %param.18) | copy-start | bytes 8650756
  22.9 170.9 %all-gather.5.cloned.1.call-start = ((), (), s32[]{:S(2)}) async-start(), calls=%async_computation.4 | async-start | bytes 4325376 | tf_op jit(solution)/shard_map/all_gather | solution.py:34
  64.1 4.8 copy-start.7
  64.1 6.1 %copy-start.6 = (f32[8,64,128]{2,1,0:T(8,128)S(1)}, f32[8,64,128]{2,1,0:T(8,128)}, u32[]{:S(2)}) copy-start(f32[8,64,128]{2,1,0:T(8,128)} %all_gather.13) | copy-start | bytes 786436
  145.0 148.3 %reduce-scatter.5.cloned.1.call-start = ((), (), s32[]{:S(2)}) async-start(), calls=%async_computation.5 | async-start | bytes 4325376 | tf_op jit(solution)/shard_map/reduce_scatter | solution.py:87
  197.7 4.9 copy-start.3
  197.7 4.9 %copy-start.8 = (f32[4,128,128]{2,1,0:T(8,128)S(1)}, f32[4,128,128]{2,1,0:T(8,128)}, u32[]{:S(2)}) copy-start(f32[4,128,128]{2,1,0:T(8,128)} %param.17) | copy-start | bytes 786436
  197.7 5.6 %copy-start.5 = (f32[8,64,128]{2,1,0:T(8,128)S(1)}, f32[8,64,128]{2,1,0:T(8,128)}, u32[]{:S(2)}) copy-start(f32[8,64,128]{2,1,0:T(8,128)} %all_gather.15) | copy-start | bytes 786436
  197.7 6.2 %copy-start.2 = (f32[4,11,128,64]{2,3,1,0:T(8,128)S(1)}, f32[4,11,128,64]{2,3,1,0:T(8,128)}, u32[]{:S(2)}) copy-start(f32[4,11,128,64]{2,3,1,0:T(8,128)} %fusion.2) | copy-start | bytes 4325380
  213.5 228.1 %all-reduce.2.cloned.1.call-start = ((), (), s32[]{:S(2)}) async-start(), calls=%async_computation.6 | async-start | bytes 262144 | tf_op jit(solution)/shard_map/psum | solution.py:92
  294.5 192.4 %copy-start.9 = (f32[4,64,128]{2,1,0:T(8,128)S(1)}, f32[4,64,128]{2,1,0:T(8,128)}, u32[]{:S(2)}) copy-start(f32[4,64,128]{2,1,0:T(8,128)} %reduce-scatter.5.cloned.1.call-done) | copy-start | bytes 393220
Sparse Core Ops, SparseCore 0:
  10.2 49.7 all-gather.2
  63.7 79.6 reduce-scatter.2
  146.2 47.5 all-gather.4
  213.6 79.7 reduce-scatter.4
  298.5 142.9 all-reduce.1
where the time goes:
time: 496 us; the launch traced here: 495 us
  waiting for transfers between devices  343 us (69%)
  other arithmetic  55.1 us (11%)
  matrix products  30.5 us (6%)
  local copies, waits for them, and re-layouts  28.1 us (6%)
  blocking collectives  23.2 us (5%)
  between operations  14.3 us (3%)
    psum x1, waiting for transfers between devices, local(): grams = lax.psum(grams, ('group', 'bulk'))  146 us
    reduce_scatter x1, waiting for transfers between devices, local(): u2 = lax.psum_scatter(buffer, 'bulk', scatter_dimension=0, tiled=True)  72.2 us
    reduce_scatter x1, waiting for transfers between devices, local(): u1 = own + lax.psum_scatter(buffer, 'bulk', scatter_dimension=0, tiled=True)  71 us
    all_gather x2, waiting for transfers between devices, off_part(): panel = lax.all_gather(vectors, 'bulk', axis=0, tiled=True)  52.9 us
    all_gather x2, blocking collectives, off_part(): lax.all_gather(vectors[:boundary_rows], 'group', axis=0, tiled=True)  23.2 us
    another operation x9, other arithmetic, chol_apply(): factor = jnp.linalg.cholesky(matrix)  19.6 us
    another operation x6, other arithmetic, chol_apply(): lax.linalg.triangular_solve(factor, middle, left_side=True, lower=True, t...  16.6 us
  transfers between devices with their start and end apart: 5, of which 5 were waited for; matrix products, arithmetic and copies ran while one was open for 9% of the time, Pallas kernels for 0%

commit v1 on v0

--- a/solution.py
+++ b/solution.py
@@ -31,7 +31,10 @@
     border = lax.all_gather(vectors[:boundary_rows], "group", axis=0, tiled=True)
     own = jnp.einsum("rnj,rij->rni", vectors, diag, precision=highest)
     returned = jnp.einsum("rni,rkij->rknj", vectors, masked, precision=highest)
-    panel = lax.all_gather(vectors, "bulk", axis=0, tiled=True)
+    count = lax.axis_size("bulk")
+    shards = jnp.stack([vectors for _ in range(count)])
+    shards = lax.all_to_all(shards, "bulk", split_axis=0, concat_axis=0)
+    panel = jnp.concatenate(shards, axis=0)
     picked = panel[column_ids]
     own = own + jnp.einsum("rknj,rkij->rni", picked, masked, precision=highest)
     border = border.reshape((part_count, boundary_rows) + vectors.shape[1:])

time: 496 us -> 480 us (0.968)
  waiting for transfers between devices: 343 us -> 305 us
  starting transfers between devices: 0.2 us -> 17.3 us
    all_to_all x0 -> x2, waiting for transfers between devices: none -> 73.7 us  [off_part(): shards = lax.all_to_all(shards, 'bulk', split_axis=0, concat_axis=0)]
    reduce_scatter x1, waiting for transfers between devices: 71 us -> 12.4 us  [local(): u1 = own + lax.psum_scatter(buffer, 'bulk', scatter_dimension=0, tiled=True)]
    all_gather x2 -> x0, waiting for transfers between devices: 52.9 us -> none  [off_part(): panel = lax.all_gather(vectors, 'bulk', axis=0, tiled=True)]
    all_to_all x0 -> x2, starting transfers between devices: none -> 17.2 us  [off_part(): shards = lax.all_to_all(shards, 'bulk', split_axis=0, concat_axis=0)]
    another operation x2 -> x4, local copies, waits for them, and re-layouts: 5 us -> 10 us
  transfers between devices with their start and end apart: 5 -> 5, of which waited for: 5 -> 5; matrix products, arithmetic and copies ran while one was open for 9% -> 6% of each run, Pallas kernels for 0% -> 0%
where the time goes in v1:
time: 480 us; the launch traced here: 479 us
  waiting for transfers between devices  305 us (64%)
  other arithmetic  55.6 us (12%)
  local copies, waits for them, and re-layouts  32.9 us (7%)
  matrix products  29.6 us (6%)
  blocking collectives  24 us (5%)
  starting transfers between devices  17.3 us (4%)
  between operations  14.3 us (3%)
    psum x1, waiting for transfers between devices, local(): grams = lax.psum(grams, ('group', 'bulk'))  147 us
    all_to_all x2, waiting for transfers between devices, off_part(): shards = lax.all_to_all(shards, 'bulk', split_axis=0, concat_axis=0)  73.7 us
    reduce_scatter x1, waiting for transfers between devices, local(): u2 = lax.psum_scatter(buffer, 'bulk', scatter_dimension=0, tiled=True)  72.6 us
    all_gather x2, blocking collectives, off_part(): lax.all_gather(vectors[:boundary_rows], 'group', axis=0, tiled=True)  24 us
    another operation x9, other arithmetic, chol_apply(): factor = jnp.linalg.cholesky(matrix)  19.6 us
    all_to_all x2, starting transfers between devices, off_part(): shards = lax.all_to_all(shards, 'bulk', split_axis=0, concat_axis=0)  17.2 us
    another operation x6, other arithmetic, chol_apply(): lax.linalg.triangular_solve(factor, middle, left_side=True, lower=True, t...  16.6 us
    reduce_scatter x1, waiting for transfers between devices, local(): u1 = own + lax.psum_scatter(buffer, 'bulk', scatter_dimension=0, tiled=True)  12.4 us
  transfers between devices with their start and end apart: 5, of which 5 were waited for; matrix products, arithmetic and copies ran while one was open for 6% of the time, Pallas kernels for 0%

profile of v1, /device:TPU:1, one launch (start us, length us, event | category | flops | bytes accessed | tf_op | source)
XLA Modules:
  0.0 478.9 jit_solution(547046562067172385)
XLA Ops:
  7.2 0.8 dynamic_slice.22
  8.1 0.8 compare_select_fusion
  9.6 3.8 fusion.4
  13.4 2.5 broadcast.144.clone
  15.9 6.9 %scatter_fusion = f32[128,64,128]{2,1,0:T(8,128)} fusion(f32[128,64,128]{2,1,0:T(8,128)} %broadcast.144.clone, s32[44]{0:T(128)S(1)} %reshape.218, f32[44,64,128]{2,1,0:T(8,128)S(1)} %bitcast.250), kind=kCustom, calls=%fused_computation.6 | custom fusion | flops 360448 | bytes 4325552 | tf_op jit(solution)/shard_map/scatter-add | solution.py:85
  22.8 0.9 copy-done.3
  23.7 2.5 stack.14
  26.2 9.7 %all-to-all-start = ((f32[32,4,64,128]{3,2,1,0:T(8,128)}), f32[32,4,64,128]{3,2,1,0:T(8,128)}, u32[]{:S(2)}, u32[]{:S(2)}) async-start(f32[32,4,64,128]{3,2,1,0:T(8,128)} %stack.14), calls=%async_computation | async-start | bytes 8388608 | tf_op jit(solution)/shard_map/all_to_all | solution.py:36
  36.7 12.6 %all_gather.6 = f32[8,64,128]{2,1,0:T(8,128)} all-gather(f32[2,64,128]{2,1,0:T(8,128)} %slice.81), channel_id=1, replica_groups=mesh['group'=4,'bulk'=32] {'group'}, dimensions={0}, use_global_device_ids=true | all-gather | bytes 327680 | tf_op jit(solution)/shard_map/all_gather | solution.py:31
  49.3 41.7 %all-to-all-done = f32[32,4,64,128]{3,2,1,0:T(8,128)} async-done(((f32[32,4,64,128]{3,2,1,0:T(8,128)}), f32[32,4,64,128]{3,2,1,0:T(8,128)}, u32[]{:S(2)}, u32[]{:S(2)}) %all-to-all-start) | async-done | bytes 4194336 | tf_op jit(solution)/shard_map/all_to_all | solution.py:36
  90.9 4.0 gather_fusion.1
  94.9 4.9 %fusion.12 = f32[4,64,128]{2,1,0:T(8,128)S(1)} fusion(f32[4,11,64,128]{3,2,1,0:T(8,128)} %bitcast.252, f32[4,11,128,128]{3,2,1,0:T(8,128)S(1)} %copy-done.1, f32[4,11]{1,0:T(4,128)S(1)} %fusion.85), kind=kOutput, calls=%fused_computation.22 | convolution fusion | flops 554369024 | bytes 4456624 | tf_op jit(solution)/shard_map/rknj,rkij->rni/dot_general | solution.py:39
  99.8 1.3 convolution_add_fusion.1
  101.1 2.1 fusion.21
  103.2 12.4 %reduce-scatter.3.cloned.1.call-done = f32[4,64,128]{2,1,0:T(8,128)} async-done(((f32[128,64,128]{2,1,0:T(8,128)}), f32[4,64,128]{2,1,0:T(8,128)}) %reduce-scatter.3.cloned.1.call-update) | async-done | bytes 131088 | tf_op jit(solution)/shard_map/reduce_scatter | solution.py:86
  115.6 1.0 add.181
  116.6 2.5 stack.15
  119.1 7.5 %all-to-all-start.1 = ((f32[32,4,64,128]{3,2,1,0:T(8,128)}), f32[32,4,64,128]{3,2,1,0:T(8,128)}, u32[]{:S(2)}, u32[]{:S(2)}) async-start(f32[32,4,64,128]{3,2,1,0:T(8,128)} %stack.15), calls=%async_computation.2 | async-start | bytes 8388608 | tf_op jit(solution)/shard_map/all_to_all | solution.py:36
  126.8 1.3 compare_select_fusion.3
  128.6 1.3 gather_fusion.3
  130.0 0.7 pad_add_fusion
  130.7 11.5 %all_gather.7 = f32[8,64,128]{2,1,0:T(8,128)} all-gather(f32[2,64,128]{2,1,0:T(8,128)S(1)} %slice.102), channel_id=1, replica_groups=mesh['group'=4,'bulk'=32] {'group'}, dimensions={0}, use_global_device_ids=true | all-gather | bytes 327680 | tf_op jit(solution)/shard_map/all_gather | solution.py:31
  142.1 3.2 fusion.2
  145.3 32.0 %all-to-all-done.1 = f32[32,4,64,128]{3,2,1,0:T(8,128)} async-done(((f32[32,4,64,128]{3,2,1,0:T(8,128)}), f32[32,4,64,128]{3,2,1,0:T(8,128)}, u32[]{:S(2)}, u32[]{:S(2)}) %all-to-all-start.1) | async-done | bytes 4194336 | tf_op jit(solution)/shard_map/all_to_all | solution.py:36
  177.3 4.0 gather_fusion.4
  181.3 4.9 %fusion.15 = f32[4,64,128]{2,1,0:T(8,128)S(1)} fusion(f32[4,11,64,128]{3,2,1,0:T(8,128)} %bitcast.251, f32[4,11,128,128]{3,2,1,0:T(8,128)S(1)} %copy-done.1, f32[4,11]{1,0:T(4,128)S(1)} %fusion.85), kind=kOutput, calls=%fused_computation.23 | convolution fusion | flops 554369024 | bytes 4456624 | tf_op jit(solution)/shard_map/rknj,rkij->rni/dot_general | solution.py:39
  186.9 0.7 fusion.19
  187.7 2.5 broadcast.144
  190.2 6.9 %scatter_fusion.1 = f32[128,64,128]{2,1,0:T(8,128)} fusion(f32[128,64,128]{2,1,0:T(8,128)} %broadcast.144, s32[48]{0:T(128)S(1)} %pad_add_fusion, f32[48,64,128]{2,1,0:T(8,128)S(1)} %pad_maximum_fusion), kind=kCustom, calls=%fused_computation.7 | custom fusion | flops 393216 | bytes 4718784 | tf_op jit(solution)/shard_map/scatter-add | solution.py:89
  197.2 1.3 scatter_custom_fusion
  198.6 2.7 gather_fusion
  201.6 2.7 gather_fusion.2
  204.9 72.6 %reduce-scatter.5.cloned.1.call-done = f32[4,64,128]{2,1,0:T(8,128)} async-done(((f32[128,64,128]{2,1,0:T(8,128)}), f32[4,64,128]{2,1,0:T(8,128)}) %reduce-scatter.5.cloned.1.call-update) | async-done | bytes 131088 | tf_op jit(solution)/shard_map/reduce_scatter | solution.py:90
  277.4 1.2 convolution_bitcast_fusion.3
  278.6 0.7 pad_maximum_fusion.1
  279.3 146.5 %all-reduce.2.cloned.1.call-done = f32[4,64,64]{2,1,0:T(8,128)} async-done(((f32[4,64,64]{2,1,0:T(8,128)}), f32[4,64,64]{2,1,0:T(8,128)}) %all-reduce.2.cloned.1.call-update) | async-done | bytes 65552 | tf_op jit(solution)/shard_map/psum | solution.py:95
  425.8 0.8 slice_bitcast_fusion.2
  426.8 0.8 multiply_add_fusion
  427.9 5.9 %cholesky.59 = f32[64,64]{1,0:T(8,128)S(1)} custom-call(f32[64,64]{1,0:T(8,128)S(1)} %copy.82), custom_call_target="Cholesky" | custom-call | tf_op jit(solution)/shard_map/jit(cholesky)/cholesky | solution.py:11
  434.4 0.7 fusion.41
  435.1 4.9 %custom-call.13 = f32[1,64,64]{1,2,0:T(8,128)S(1)} custom-call(f32[1,64,64]{2,1,0:T(8,128)S(1)} %fusion.41), custom_call_target="InvertDiagBlocksLowerTriangular" | custom-call | tf_op jit(solution)/shard_map/triangular_solve/custom-call.2 | solution.py:13
  441.0 5.9 %cholesky.70 = f32[64,64]{1,0:T(8,128)S(1)} custom-call(f32[64,64]{1,0:T(8,128)S(1)} %copy.85), custom_call_target="Cholesky" | custom-call | tf_op jit(solution)/shard_map/jit(cholesky)/cholesky | solution.py:11
  448.2 4.9 %custom-call.15 = f32[1,64,64]{1,2,0:T(8,128)S(1)} custom-call(f32[1,64,64]{2,1,0:T(8,128)S(1)} %fusion.42), custom_call_target="InvertDiagBlocksLowerTriangular" | custom-call | tf_op jit(solution)/shard_map/triangular_solve/custom-call.2 | solution.py:13
  453.1 1.0 fusion.67
  456.1 1.0 fusion.45
  458.2 5.8 %cholesky.81 = f32[64,64]{1,0:T(8,128)S(1)} custom-call(f32[64,64]{1,0:T(8,128)S(1)} %fusion.51), custom_call_target="Cholesky" | custom-call | tf_op jit(solution)/shard_map/jit(cholesky)/cholesky | solution.py:11
  465.4 4.9 %custom-call.17 = f32[1,64,64]{1,2,0:T(8,128)S(1)} custom-call(f32[1,64,64]{2,1,0:T(8,128)S(1)} %fusion.43), custom_call_target="InvertDiagBlocksLowerTriangular" | custom-call | tf_op jit(solution)/shard_map/triangular_solve/custom-call.2 | solution.py:13
  471.7 0.7 fusion.103
  (98 shorter events, 13.2 us)
Async XLA Ops:
  7.2 93.9 %copy-start = (f32[2,4,128,128]{3,2,1,0:T(8,128)S(1)}, f32[2,4,128,128]{3,2,1,0:T(8,128)}, u32[]{:S(2)}) copy-start(f32[2,4,128,128]{3,2,1,0:T(8,128)} %param.19) | copy-start | bytes 1572868
  7.2 108.4 %reduce-scatter.3.cloned.1.call-start = ((), (), s32[]{:S(2)}) async-start(), calls=%async_computation.4 | async-start | bytes 4325376 | tf_op jit(solution)/shard_map/reduce_scatter | solution.py:86
  9.0 0.6 copy-start.9
  22.8 0.9 copy-start.3
  26.2 64.7 %all-to-all-start = ((f32[32,4,64,128]{3,2,1,0:T(8,128)}), f32[32,4,64,128]{3,2,1,0:T(8,128)}, u32[]{:S(2)}, u32[]{:S(2)}) async-start(f32[32,4,64,128]{3,2,1,0:T(8,128)} %stack.14), calls=%async_computation | async-start | bytes 8388608 | tf_op jit(solution)/shard_map/all_to_all | solution.py:36
  35.9 59.0 %copy-start.1 = (f32[4,11,128,128]{3,2,1,0:T(8,128)S(1)}, f32[4,11,128,128]{3,2,1,0:T(8,128)}, u32[]{:S(2)}) copy-start(f32[4,11,128,128]{3,2,1,0:T(8,128)} %param.18) | copy-start | bytes 8650756
  94.9 4.9 %copy-start.6 = (f32[4,128,128]{2,1,0:T(8,128)S(1)}, f32[4,128,128]{2,1,0:T(8,128)}, u32[]{:S(2)}) copy-start(f32[4,128,128]{2,1,0:T(8,128)} %param.17) | copy-start | bytes 786436
  94.9 6.2 %copy-start.5 = (f32[8,64,128]{2,1,0:T(8,128)S(1)}, f32[8,64,128]{2,1,0:T(8,128)}, u32[]{:S(2)}) copy-start(f32[8,64,128]{2,1,0:T(8,128)} %all_gather.6) | copy-start | bytes 786436
  119.1 7.6 %copy-start.10 = (s32[4,11]{1,0:T(4,128)S(1)}, s32[4,11]{1,0:T(4,128)}, u32[]{:S(2)}) copy-start(s32[4,11]{1,0:T(4,128)} %copy-done.9) | copy-start | bytes 532
  119.1 58.2 %all-to-all-start.1 = ((f32[32,4,64,128]{3,2,1,0:T(8,128)}), f32[32,4,64,128]{3,2,1,0:T(8,128)}, u32[]{:S(2)}, u32[]{:S(2)}) async-start(f32[32,4,64,128]{3,2,1,0:T(8,128)} %stack.15), calls=%async_computation.2 | async-start | bytes 8388608 | tf_op jit(solution)/shard_map/all_to_all | solution.py:36
  126.6 150.8 %reduce-scatter.5.cloned.1.call-start = ((), (), s32[]{:S(2)}) async-start(), calls=%async_computation.5 | async-start | bytes 4325376 | tf_op jit(solution)/shard_map/reduce_scatter | solution.py:90
  181.3 4.9 %copy-start.7 = (f32[4,128,128]{2,1,0:T(8,128)S(1)}, f32[4,128,128]{2,1,0:T(8,128)}, u32[]{:S(2)}) copy-start(f32[4,128,128]{2,1,0:T(8,128)} %param.17) | copy-start | bytes 786436
  181.3 5.6 %copy-start.4 = (f32[8,64,128]{2,1,0:T(8,128)S(1)}, f32[8,64,128]{2,1,0:T(8,128)}, u32[]{:S(2)}) copy-start(f32[8,64,128]{2,1,0:T(8,128)} %all_gather.7) | copy-start | bytes 786436
  181.3 6.2 %copy-start.2 = (f32[4,11,128,64]{2,3,1,0:T(8,128)S(1)}, f32[4,11,128,64]{2,3,1,0:T(8,128)}, u32[]{:S(2)}) copy-start(f32[4,11,128,64]{2,3,1,0:T(8,128)} %fusion.2) | copy-start | bytes 4325380
  197.1 228.7 %all-reduce.2.cloned.1.call-start = ((), (), s32[]{:S(2)}) async-start(), calls=%async_computation.6 | async-start | bytes 262144 | tf_op jit(solution)/shard_map/psum | solution.py:95
  278.6 192.6 %copy-start.8 = (f32[4,64,128]{2,1,0:T(8,128)S(1)}, f32[4,64,128]{2,1,0:T(8,128)}, u32[]{:S(2)}) copy-start(f32[4,64,128]{2,1,0:T(8,128)} %reduce-scatter.5.cloned.1.call-done) | copy-start | bytes 393220
Sparse Core Ops, SparseCore 0:
  23.0 92.6 reduce-scatter.2
  197.2 80.1 reduce-scatter.4
  282.7 143.0 all-reduce.1
